TPU v7x, 32 devices: a whole 2x2x4 slice. The times are simulated.
32 devices in a mesh: pair: 8 (over z, x), rows: 4 (over y, core).
Axes of the slice: x: 2, y: 2, z: 4, core: 2. Of those that a mesh axis runs over, the one named last changes fastest.
Arguments:
- matrix: float32 [16384, 2048], P('rows', 'pair')
- plan: int32 [3, 8], P(None, 'pair'), may hold values 0 or 1
Outputs:
- rotated: float32 [16384, 2048], P('rows', 'pair')
- offness: float32 [3], replicated
All inputs are finite; a program needn't handle non-finite values. No bound on the sum of `plan` on one device may be relied on, other than what follows from the above.
Results may differ from a plain program's by a relative error of at most 0.00025.
Values sent between devices are 32-bit elements; how exact they have to be, the bound alone decides.
A program may use at most 64 MiB of HBM per device.

v0:
```python
import jax
import jax.numpy as jnp
from jax import lax
from jax.sharding import PartitionSpec as P

ROUNDS = 3


def from_behind(x, axis, by):
    peers = lax.axis_size(axis)
    return lax.ppermute(x, axis, [(i, (i + by) % peers) for i in range(peers)])


def off_total(value):
    return lax.psum(value, "pair")


def pass_on(block):
    return from_behind(block, "pair", 1)


def make_rotation(gram, mean_sq, eye, weights):
    diagonal = jnp.diagonal(gram)
    denom = diagonal[:, None] + diagonal[None, :] + mean_sq
    skew = gram * (weights[None, :] - weights[:, None]) / denom
    square = jnp.dot(skew, skew, precision=lax.Precision.HIGHEST)
    plus = eye + skew
    numer = jnp.dot(plus, plus, precision=lax.Precision.HIGHEST)
    lower = jnp.linalg.cholesky(eye - square)
    return jax.scipy.linalg.cho_solve((lower, True), numer)


def local(matrix, plan):
    width = matrix.shape[1]
    half = width // 2
    pair_count = lax.axis_size("pair")
    ncols_all = width * pair_count
    eye = jnp.eye(width, dtype=jnp.float32)
    weights = jnp.arange(width, dtype=jnp.float32) / jnp.float32(width - 1)
    mean_sq = lax.psum(jnp.sum(matrix * matrix), ("pair", "rows")) / ncols_all
    current = matrix
    values = []
    for step in range(ROUNDS):
        partial_gram = lax.dot_general(
            current,
            current,
            (((0,), (0,)), ((), ())),
            precision=lax.Precision.HIGHEST,
            preferred_element_type=jnp.float32,
        )
        gram = lax.psum(partial_gram, "rows")
        offdiag = gram * (1.0 - eye)
        off_local = jnp.sum(offdiag * offdiag)
        if step == 0:
            total_off = off_total(off_local)
        else:
            total_off = off_total(off_local)
        values.append(jnp.sqrt(total_off / (pair_count * width * (width - 1))) / mean_sq)
        rotation = make_rotation(gram, mean_sq, eye, weights)
        keep_last = plan[step, 0] == 1
        turned = jnp.dot(current, rotation, precision=lax.Precision.HIGHEST)
        first_half = turned[:, :half]
        second_half = turned[:, half:]
        kept = jnp.where(keep_last, second_half, first_half)
        moving = jnp.where(keep_last, first_half, second_half)
        arrived = pass_on(moving)
        current = jnp.concatenate([kept, arrived], axis=1)
    return (current, jnp.stack(values))


def solution(mesh):
    in_specs = (P("rows", "pair"), P(None, "pair"))
    out_specs = (P("rows", "pair"), P())
    return jax.shard_map(local, mesh=mesh, in_specs=in_specs, out_specs=out_specs, check_vma=False)
```

profile of v0, /device:TPU:0, one launch (start us, length us, event | category | flops | bytes accessed | tf_op | source)
XLA Modules:
  0.0 539.2 jit_solution(11518162019927558470)
XLA Ops:
  7.2 10.9 %fusion.76 = f32[256,256]{0,1:T(8,128)} fusion(f32[4096,256]{1,0:T(8,128)} %param.5), kind=kOutput, calls=%fused_computation.150 | convolution fusion | flops 3221225472 | bytes 4456448 | tf_op jit(solution)/shard_map/dot_general | solution.py:44
  18.2 3.9 multiply_reduce_fusion
  22.7 42.5 %psum.50 = f32[]{:T(128)} all-reduce(f32[]{:T(128)} %multiply_reduce_fusion), channel_id=1, replica_groups=mesh['pair'=8,'rows'=4] {'pair','rows'}, use_global_device_ids=true, to_apply=%region_2.0 | all-reduce | flops 1 | bytes 8 | tf_op jit(solution)/shard_map/psum | solution.py:40
  71.0 11.7 %cholesky.172 = f32[128,128]{1,0:T(8,128)S(1)} custom-call(f32[128,128]{1,0:T(8,128)S(1)} %cholesky.270), custom_call_target="Cholesky" | custom-call | tf_op jit(solution)/shard_map/jit(cholesky)/cholesky | solution.py:29
  82.8 9.8 %custom-call.23 = f32[1,128,128]{1,2,0:T(8,128)S(1)} custom-call(f32[1,128,128]{2,1,0:T(8,128)S(1)} %get-tuple-element.81), custom_call_target="InvertDiagBlocksLowerTriangular" | custom-call | tf_op jit(solution)/shard_map/jit(cholesky)/cholesky | solution.py:29
  93.1 11.7 %cholesky.189 = f32[128,128]{1,0:T(8,128)S(1)} custom-call(f32[128,128]{1,0:T(8,128)S(1)} %convolution_subtract_fusion.11), custom_call_target="Cholesky" | custom-call | tf_op jit(solution)/shard_map/jit(cholesky)/cholesky | solution.py:29
  106.9 4.0 while.6
  110.9 19.8 %custom-call.24 = f32[2,128,128]{1,2,0:T(8,128)S(1)} custom-call(f32[2,128,128]{2,1,0:T(8,128)S(1)} %get-tuple-element.24), custom_call_target="InvertDiagBlocksLowerTriangular" | custom-call | tf_op jit(solution)/shard_map/jit(_cho_solve)/triangular_solve | solution.py:30
  133.3 8.8 %convolution_bitcast_fusion = f32[4096,256]{0,1:T(8,128)S(1)} fusion(f32[4096,256]{1,0:T(8,128)} %param.5, f32[128,256]{1,0:T(8,128)S(1)} %fusion.47, f32[128,256]{1,0:T(8,128)S(1)} %fusion.46), kind=kOutput, calls=%fused_computation.9 | convolution fusion | flops 3221291008 | bytes 8650752 | tf_op jit(solution)/shard_map/dot_general | solution.py:61
  144.8 47.0 %collective-permute-done = f32[4096,128]{0,1:T(8,128)S(1)} collective-permute-done((f32[4096,128]{0,1:T(8,128)S(1)}, f32[4096,128]{0,1:T(8,128)S(1)}, u32[]{:S(2)}, u32[]{:S(2)}) %collective-permute-start) | collective-permute-done | bytes 2097184 | tf_op jit(solution)/shard_map/ppermute | solution.py:11
  193.1 4.2 fusion.3
  198.2 28.8 %all-reduce.8.cloned.1.call-done = f32[256,256]{0,1:T(8,128)} async-done(((f32[256,256]{0,1:T(8,128)}), f32[256,256]{0,1:T(8,128)}) %all-reduce.8.cloned.1.call-update) | async-done | bytes 262160 | tf_op jit(solution)/shard_map/psum | solution.py:51
  227.0 2.7 gather_fusion.1
  231.4 11.7 %cholesky.206 = f32[128,128]{1,0:T(8,128)S(1)} custom-call(f32[128,128]{1,0:T(8,128)S(1)} %cholesky.273), custom_call_target="Cholesky" | custom-call | tf_op jit(solution)/shard_map/jit(cholesky)/cholesky | solution.py:29
  243.9 9.8 %custom-call.25 = f32[1,128,128]{1,2,0:T(8,128)S(1)} custom-call(f32[1,128,128]{2,1,0:T(8,128)S(1)} %get-tuple-element.77), custom_call_target="InvertDiagBlocksLowerTriangular" | custom-call | tf_op jit(solution)/shard_map/jit(cholesky)/cholesky | solution.py:29
  254.2 11.7 %cholesky.223 = f32[128,128]{1,0:T(8,128)S(1)} custom-call(f32[128,128]{1,0:T(8,128)S(1)} %convolution_subtract_fusion.10), custom_call_target="Cholesky" | custom-call | tf_op jit(solution)/shard_map/jit(cholesky)/cholesky | solution.py:29
  268.0 4.5 while.7
  272.5 19.7 %custom-call.26 = f32[2,128,128]{1,2,0:T(8,128)S(1)} custom-call(f32[2,128,128]{2,1,0:T(8,128)S(1)} %get-tuple-element.25), custom_call_target="InvertDiagBlocksLowerTriangular" | custom-call | tf_op jit(solution)/shard_map/jit(_cho_solve)/triangular_solve | solution.py:30
  294.7 4.0 fusion.2
  300.7 47.2 %collective-permute-done.1 = f32[4096,128]{0,1:T(8,128)S(1)} collective-permute-done((f32[4096,128]{0,1:T(8,128)S(1)}, f32[4096,128]{0,1:T(8,128)S(1)}, u32[]{:S(2)}, u32[]{:S(2)}) %collective-permute-start.1) | collective-permute-done | bytes 2097184 | tf_op jit(solution)/shard_map/ppermute | solution.py:11
  349.3 4.2 fusion.1
  354.1 29.9 %all-reduce.10.cloned.1.call-done = f32[256,256]{0,1:T(8,128)} async-done(((f32[256,256]{0,1:T(8,128)}), f32[256,256]{0,1:T(8,128)}) %all-reduce.10.cloned.1.call-update) | async-done | bytes 262160 | tf_op jit(solution)/shard_map/psum | solution.py:51
  384.0 2.7 gather_fusion.2
  389.1 11.7 %cholesky.240 = f32[128,128]{1,0:T(8,128)S(1)} custom-call(f32[128,128]{1,0:T(8,128)S(1)} %cholesky.276), custom_call_target="Cholesky" | custom-call | tf_op jit(solution)/shard_map/jit(cholesky)/cholesky | solution.py:29
  401.5 9.8 %custom-call.27 = f32[1,128,128]{1,2,0:T(8,128)S(1)} custom-call(f32[1,128,128]{2,1,0:T(8,128)S(1)} %get-tuple-element.73), custom_call_target="InvertDiagBlocksLowerTriangular" | custom-call | tf_op jit(solution)/shard_map/jit(cholesky)/cholesky | solution.py:29
  413.5 11.9 %cholesky.257 = f32[128,128]{1,0:T(8,128)S(1)} custom-call(f32[128,128]{1,0:T(8,128)S(1)} %convolution_subtract_fusion.9), custom_call_target="Cholesky" | custom-call | tf_op jit(solution)/shard_map/jit(cholesky)/cholesky | solution.py:29
  427.4 3.8 while.8
  431.2 19.7 %custom-call.28 = f32[2,128,128]{1,2,0:T(8,128)S(1)} custom-call(f32[2,128,128]{2,1,0:T(8,128)S(1)} %get-tuple-element.26), custom_call_target="InvertDiagBlocksLowerTriangular" | custom-call | tf_op jit(solution)/shard_map/jit(_cho_solve)/triangular_solve | solution.py:30
  453.5 4.0 fusion
  462.7 57.4 %all-reduce.1 = (f32[]{:T(128)}, f32[]{:T(128)}, f32[]{:T(128)}) all-reduce(f32[]{:T(128)} %fusion.12, f32[]{:T(128)} %fusion.10, f32[]{:T(128)} %fusion.8), channel_id=1, replica_groups=mesh['pair'=8,'rows'=4] {'pair'}, use_global_device_ids=true, to_apply=%region_14.17 | all-reduce | flops 3 | bytes 24 | tf_op jit(solution)/shard_map/psum | solution.py:15
  522.9 3.9 pad_maximum_fusion.2
  526.8 5.6 %copy.23 = f32[4096,256]{1,0:T(8,128)} copy(f32[4096,256]{0,1:T(8,128)} %pad_maximum_fusion.2) | data formatting | bytes 8388608
  (119 shorter events, 48.9 us)
Async XLA Ops:
  7.2 59.4 %all-reduce.6.cloned.1.call-start = ((), (), s32[]{:S(2)}) async-start(), calls=%async_computation | async-start | bytes 524288 | tf_op jit(solution)/shard_map/psum | solution.py:51
  18.1 4.0 copy-start.8
  18.1 208.9 %all-reduce.8.cloned.1.call-start = ((), (), s32[]{:S(2)}) async-start(), calls=%async_computation.1 | async-start | bytes 524288 | tf_op jit(solution)/shard_map/psum | solution.py:51
  66.6 64.2 %copy-start = (f32[256,256]{0,1:T(8,128)S(1)}, f32[256,256]{0,1:T(8,128)}, u32[]{:S(2)}) copy-start(f32[256,256]{0,1:T(8,128)} %all-reduce.6.cloned.1.call-done) | copy-start | bytes 786436
  142.5 49.3 %collective-permute-start = (f32[4096,128]{0,1:T(8,128)S(1)}, f32[4096,128]{0,1:T(8,128)S(1)}, u32[]{:S(2)}, u32[]{:S(2)}) collective-permute-start(f32[4096,128]{0,1:T(8,128)S(1)} %get-tuple-element.69), channel_id=1, source_target_pairs={{0,4},{4,8},{8,12},{12,16},{16,20},{20,24},{24,28},{28,0},{1,5},{5... | collective-permute-start | bytes 6291464 | tf_op jit(solution)/shard_map/ppermute | solution.py:11
  191.8 1.3 copy-start.5
  197.3 186.7 %all-reduce.10.cloned.1.call-start = ((), (), s32[]{:S(2)}) async-start(), calls=%async_computation.2 | async-start | bytes 524288 | tf_op jit(solution)/shard_map/psum | solution.py:51
  227.0 65.1 %copy-start.1 = (f32[256,256]{0,1:T(8,128)S(1)}, f32[256,256]{0,1:T(8,128)}, u32[]{:S(2)}) copy-start(f32[256,256]{0,1:T(8,128)} %all-reduce.8.cloned.1.call-done) | copy-start | bytes 786436
  292.1 2.5 copy-start.6
  299.0 48.9 %collective-permute-start.1 = (f32[4096,128]{0,1:T(8,128)S(1)}, f32[4096,128]{0,1:T(8,128)S(1)}, u32[]{:S(2)}, u32[]{:S(2)}) collective-permute-start(f32[4096,128]{0,1:T(8,128)S(1)} %get-tuple-element.67), channel_id=1, source_target_pairs={{0,4},{4,8},{8,12},{12,16},{16,20},{20,24},{24,28},{28,0},{1,5},{5... | collective-permute-start | bytes 6291464 | tf_op jit(solution)/shard_map/ppermute | solution.py:11
  348.0 1.3 copy-start.3
  384.0 66.9 %copy-start.2 = (f32[256,256]{0,1:T(8,128)S(1)}, f32[256,256]{0,1:T(8,128)}, u32[]{:S(2)}) copy-start(f32[256,256]{0,1:T(8,128)} %all-reduce.10.cloned.1.call-done) | copy-start | bytes 786436
  388.4 0.7 copy-start.7
  450.9 2.5 copy-start.4
  459.2 63.7 %collective-permute-start.2 = (f32[4096,128]{0,1:T(8,128)}, f32[4096,128]{0,1:T(8,128)}, u32[]{:S(2)}, u32[]{:S(2)}) collective-permute-start(f32[4096,128]{0,1:T(8,128)} %get-tuple-element.65), channel_id=1, source_target_pairs={{0,4},{4,8},{8,12},{12,16},{16,20},{20,24},{24,28},{28,0},{1,5},{5... | collective-permute-start | bytes 6291464 | tf_op jit(solution)/shard_map/ppermute | solution.py:11
Sparse Core Ops, SparseCore 0:
  18.2 35.0 all-reduce.5
  197.5 29.4 all-reduce.7
  353.7 30.3 all-reduce.9
where the time goes:
time: 546 us; the launch traced here: 539 us
  other arithmetic  176 us (32%)
  waiting for transfers between devices  153 us (28%)
  blocking collectives  100 us (18%)
  matrix products  51.3 us (9%)
  local copies, waits for them, and re-layouts  29.9 us (5%)
  between operations  23 us (4%)
  starting transfers between devices  5.82 us (1%)
    another operation x20, other arithmetic, make_rotation(): lower = jnp.linalg.cholesky(eye - square)  103 us
    ppermute x3, waiting for transfers between devices, from_behind(): return lax.ppermute(x, axis, [(i, (i + by) % peers) for i in range(peers)])  94.2 us
    another operation x7, other arithmetic, make_rotation(): return jax.scipy.linalg.cho_solve((lower, True), numer)  59.3 us
    psum x3, waiting for transfers between devices, local(): gram = lax.psum(partial_gram, 'rows')  58.7 us
    psum x1, blocking collectives, off_total(): return lax.psum(value, 'pair')  57.4 us
    psum x1, blocking collectives, local(): mean_sq = lax.psum(jnp.sum(matrix * matrix), ('pair', 'rows')) / ncols_all  42.5 us
    dot_general x3, matrix products, local(): lax.dot_general(current, current, (((0,), (0,)), ((), ())), precision=lax...  19.4 us
    dot_general x3, matrix products, local(): turned = jnp.dot(current, rotation, precision=lax.Precision.HIGHEST)  16.8 us
  transfers between devices with their start and end apart: 6, of which 4 were waited for; matrix products, arithmetic and copies ran while one was open for 1% of the time, Pallas kernels for 0%

commit v1 on v0

--- a/solution.py
+++ b/solution.py
@@ -48,7 +48,8 @@
             precision=lax.Precision.HIGHEST,
             preferred_element_type=jnp.float32,
         )
-        gram = lax.psum(partial_gram, "rows")
+        shards = lax.all_gather(partial_gram, "rows", axis=0, tiled=False)
+        gram = shards.sum(axis=0)
         offdiag = gram * (1.0 - eye)
         off_local = jnp.sum(offdiag * offdiag)
         if step == 0:

time: 546 us -> 529 us (0.969)
  waiting for transfers between devices: 153 us -> 123 us
  matrix products: 51.3 us -> 57.2 us
    psum x3 -> x0, waiting for transfers between devices: 58.7 us -> none  [local(): gram = lax.psum(partial_gram, 'rows')]
    all_gather x0 -> x3, waiting for transfers between devices: none -> 26.9 us  [local(): shards = lax.all_gather(partial_gram, 'rows', axis=0, tiled=False)]
where the time goes in v1:
time: 529 us; the launch traced here: 521 us
  other arithmetic  180 us (34%)
  waiting for transfers between devices  123 us (23%)
  blocking collectives  101 us (19%)
  matrix products  57.2 us (11%)
  local copies, waits for them, and re-layouts  30.4 us (6%)
  between operations  23.2 us (4%)
  starting transfers between devices  5.43 us (1%)
    another operation x20, other arithmetic, make_rotation(): lower = jnp.linalg.cholesky(eye - square)  103 us
    ppermute x3, waiting for transfers between devices, from_behind(): return lax.ppermute(x, axis, [(i, (i + by) % peers) for i in range(peers)])  96.2 us
    another operation x7, other arithmetic, make_rotation(): return jax.scipy.linalg.cho_solve((lower, True), numer)  59.9 us
    psum x1, blocking collectives, off_total(): return lax.psum(value, 'pair')  59 us
    psum x1, blocking collectives, local(): mean_sq = lax.psum(jnp.sum(matrix * matrix), ('pair', 'rows')) / ncols_all  42.3 us
    all_gather x3, waiting for transfers between devices, local(): shards = lax.all_gather(partial_gram, 'rows', axis=0, tiled=False)  26.9 us
    dot_general x3, matrix products, local(): turned = jnp.dot(current, rotation, precision=lax.Precision.HIGHEST)  20.6 us
    dot_general x3, matrix products, local(): lax.dot_general(current, current, (((0,), (0,)), ((), ())), precision=lax...  19.4 us
  transfers between devices with their start and end apart: 6, of which 4 were waited for; matrix products, arithmetic and copies ran while one was open for 1% of the time, Pallas kernels for 0%

profile of v1, /device:TPU:0, one launch (start us, length us, event | category | flops | bytes accessed | tf_op | source)
XLA Modules:
  0.0 521.1 jit_solution(1257010163724016598)
XLA Ops:
  7.2 10.9 %fusion.76 = f32[256,256]{1,0:T(8,128)} fusion(f32[4096,256]{1,0:T(8,128)} %param.5), kind=kOutput, calls=%fused_computation.150 | convolution fusion | flops 3221225472 | bytes 4456448 | tf_op jit(solution)/shard_map/dot_general | solution.py:44
  18.2 3.9 multiply_reduce_fusion
  22.1 42.3 %psum.28 = f32[]{:T(128)} all-reduce(f32[]{:T(128)} %multiply_reduce_fusion), channel_id=1, replica_groups=mesh['pair'=8,'rows'=4] {'pair','rows'}, use_global_device_ids=true, to_apply=%region_2.0 | all-reduce | flops 1 | bytes 8 | tf_op jit(solution)/shard_map/psum | solution.py:40
  67.9 2.8 gather_fusion
  72.2 11.7 %cholesky.172 = f32[128,128]{1,0:T(8,128)S(1)} custom-call(f32[128,128]{1,0:T(8,128)S(1)} %cholesky.270), custom_call_target="Cholesky" | custom-call | tf_op jit(solution)/shard_map/jit(cholesky)/cholesky | solution.py:29
  84.0 9.8 %custom-call.23 = f32[1,128,128]{1,2,0:T(8,128)S(1)} custom-call(f32[1,128,128]{2,1,0:T(8,128)S(1)} %get-tuple-element.85), custom_call_target="InvertDiagBlocksLowerTriangular" | custom-call | tf_op jit(solution)/shard_map/jit(cholesky)/cholesky | solution.py:29
  94.3 11.7 %cholesky.189 = f32[128,128]{1,0:T(8,128)S(1)} custom-call(f32[128,128]{1,0:T(8,128)S(1)} %convolution_subtract_fusion.11), custom_call_target="Cholesky" | custom-call | tf_op jit(solution)/shard_map/jit(cholesky)/cholesky | solution.py:29
  108.1 4.0 while.6
  112.1 19.8 %custom-call.24 = f32[2,128,128]{1,2,0:T(8,128)S(1)} custom-call(f32[2,128,128]{2,1,0:T(8,128)S(1)} %get-tuple-element.24), custom_call_target="InvertDiagBlocksLowerTriangular" | custom-call | tf_op jit(solution)/shard_map/jit(_cho_solve)/triangular_solve | solution.py:30
  133.7 8.8 %convolution_bitcast_fusion = f32[4096,256]{0,1:T(8,128)S(1)} fusion(f32[4096,256]{1,0:T(8,128)} %param.5, f32[128,256]{1,0:T(8,128)S(1)} %fusion.47, f32[128,256]{1,0:T(8,128)S(1)} %fusion.46), kind=kOutput, calls=%fused_computation.9 | convolution fusion | flops 3221291008 | bytes 8650752 | tf_op jit(solution)/shard_map/dot_general | solution.py:62
  145.2 47.2 %collective-permute-done = f32[4096,128]{0,1:T(8,128)S(1)} collective-permute-done((f32[4096,128]{0,1:T(8,128)S(1)}, f32[4096,128]{0,1:T(8,128)S(1)}, u32[]{:S(2)}, u32[]{:S(2)}) %collective-permute-start) | collective-permute-done | bytes 2097184 | tf_op jit(solution)/shard_map/ppermute | solution.py:11
  193.7 4.3 fusion.3
  198.7 13.4 %all-gather.9.cloned.1.call-done = f32[1024,256]{1,0:T(8,128)} async-done(((f32[256,256]{1,0:T(8,128)}), f32[1024,256]{1,0:T(8,128)}) %all-gather.9.cloned.1.call-update) | async-done | bytes 1048592 | tf_op jit(solution)/shard_map/all_gather | solution.py:51
  213.4 2.6 gather_fusion.1
  218.3 11.7 %cholesky.206 = f32[128,128]{1,0:T(8,128)S(1)} custom-call(f32[128,128]{1,0:T(8,128)S(1)} %cholesky.273), custom_call_target="Cholesky" | custom-call | tf_op jit(solution)/shard_map/jit(cholesky)/cholesky | solution.py:29
  230.7 9.8 %custom-call.25 = f32[1,128,128]{1,2,0:T(8,128)S(1)} custom-call(f32[1,128,128]{2,1,0:T(8,128)S(1)} %get-tuple-element.81), custom_call_target="InvertDiagBlocksLowerTriangular" | custom-call | tf_op jit(solution)/shard_map/jit(cholesky)/cholesky | solution.py:29
  241.1 11.7 %cholesky.223 = f32[128,128]{1,0:T(8,128)S(1)} custom-call(f32[128,128]{1,0:T(8,128)S(1)} %convolution_subtract_fusion.10), custom_call_target="Cholesky" | custom-call | tf_op jit(solution)/shard_map/jit(cholesky)/cholesky | solution.py:29
  254.9 4.1 while.7
  259.0 20.1 %custom-call.26 = f32[2,128,128]{1,2,0:T(8,128)S(1)} custom-call(f32[2,128,128]{2,1,0:T(8,128)S(1)} %get-tuple-element.25), custom_call_target="InvertDiagBlocksLowerTriangular" | custom-call | tf_op jit(solution)/shard_map/jit(_cho_solve)/triangular_solve | solution.py:30
  282.7 5.9 %fusion.2 = f32[4096,256]{0,1:T(8,128)S(1)} fusion(f32[4096,128]{0,1:T(8,128)} %copy-done.1, f32[4096,128]{0,1:T(8,128)S(1)} %get-tuple-element.72, f32[128,256]{1,0:T(8,128)S(1)} %fusion.50, f32[128,256]{1,0:T(8,128)S(1)} %fusion.49), kind=kOutput, calls=%fused_computation.16 | convolution fusion | flops 3222339584 | bytes 8650752 | tf_op jit(solution)/shard_map/dot_general | solution.py:62
  290.5 49.0 %collective-permute-done.1 = f32[4096,128]{0,1:T(8,128)S(1)} collective-permute-done((f32[4096,128]{0,1:T(8,128)S(1)}, f32[4096,128]{0,1:T(8,128)S(1)}, u32[]{:S(2)}, u32[]{:S(2)}) %collective-permute-start.1) | collective-permute-done | bytes 2097184 | tf_op jit(solution)/shard_map/ppermute | solution.py:11
  340.8 4.3 fusion.1
  345.7 13.5 %all-gather.11.cloned.1.call-done = f32[1024,256]{1,0:T(8,128)} async-done(((f32[256,256]{1,0:T(8,128)}), f32[1024,256]{1,0:T(8,128)}) %all-gather.11.cloned.1.call-update) | async-done | bytes 1048592 | tf_op jit(solution)/shard_map/all_gather | solution.py:51
  366.1 11.7 %cholesky.240 = f32[128,128]{1,0:T(8,128)S(1)} custom-call(f32[128,128]{1,0:T(8,128)S(1)} %cholesky.276), custom_call_target="Cholesky" | custom-call | tf_op jit(solution)/shard_map/jit(cholesky)/cholesky | solution.py:29
  378.5 9.8 %custom-call.27 = f32[1,128,128]{1,2,0:T(8,128)S(1)} custom-call(f32[1,128,128]{2,1,0:T(8,128)S(1)} %get-tuple-element.77), custom_call_target="InvertDiagBlocksLowerTriangular" | custom-call | tf_op jit(solution)/shard_map/jit(cholesky)/cholesky | solution.py:29
  390.5 11.7 %cholesky.257 = f32[128,128]{1,0:T(8,128)S(1)} custom-call(f32[128,128]{1,0:T(8,128)S(1)} %convolution_subtract_fusion.9), custom_call_target="Cholesky" | custom-call | tf_op jit(solution)/shard_map/jit(cholesky)/cholesky | solution.py:29
  404.2 4.0 while.8
  408.2 19.9 %custom-call.28 = f32[2,128,128]{1,2,0:T(8,128)S(1)} custom-call(f32[2,128,128]{2,1,0:T(8,128)S(1)} %get-tuple-element.26), custom_call_target="InvertDiagBlocksLowerTriangular" | custom-call | tf_op jit(solution)/shard_map/jit(_cho_solve)/triangular_solve | solution.py:30
  431.7 5.9 %fusion = f32[4096,256]{0,1:T(8,128)S(1)} fusion(f32[4096,128]{0,1:T(8,128)} %copy-done, f32[4096,128]{0,1:T(8,128)S(1)} %get-tuple-element.70, f32[128,256]{1,0:T(8,128)S(1)} %fusion.53, f32[128,256]{1,0:T(8,128)S(1)} %fusion.52), kind=kOutput, calls=%fused_computation.14 | convolution fusion | flops 3222339584 | bytes 8650752 | tf_op jit(solution)/shard_map/dot_general | solution.py:62
  442.8 59.0 %all-reduce.1 = (f32[]{:T(128)}, f32[]{:T(128)}, f32[]{:T(128)}) all-reduce(f32[]{:T(128)} %fusion.12, f32[]{:T(128)} %fusion.10, f32[]{:T(128)} %fusion.8), channel_id=1, replica_groups=mesh['pair'=8,'rows'=4] {'pair'}, use_global_device_ids=true, to_apply=%region_14.17 | all-reduce | flops 3 | bytes 24 | tf_op jit(solution)/shard_map/psum | solution.py:15
  504.6 4.2 pad_maximum_fusion.2
  508.8 5.6 %copy.46 = f32[4096,256]{1,0:T(8,128)} copy(f32[4096,256]{0,1:T(8,128)} %pad_maximum_fusion.2) | data formatting | bytes 8388608
  (115 shorter events, 54.9 us)
Async XLA Ops:
  7.2 59.2 %all-gather.7.cloned.1.call-start = ((), (), s32[]{:S(2)}) async-start(), calls=%async_computation | async-start | bytes 1310720 | tf_op jit(solution)/shard_map/all_gather | solution.py:51
  18.1 46.9 %copy-start.3 = (s32[3,1]{0,1:T(1,128)S(1)}, s32[3,1]{0,1:T(1,128)}, u32[]{:S(2)}) copy-start(s32[3,1]{0,1:T(1,128)} %param.6) | copy-start | bytes 40
  18.2 193.9 %all-gather.9.cloned.1.call-start = ((), (), s32[]{:S(2)}) async-start(), calls=%async_computation.1 | async-start | bytes 1310720 | tf_op jit(solution)/shard_map/all_gather | solution.py:51
  142.9 49.5 %collective-permute-start = (f32[4096,128]{0,1:T(8,128)S(1)}, f32[4096,128]{0,1:T(8,128)S(1)}, u32[]{:S(2)}, u32[]{:S(2)}) collective-permute-start(f32[4096,128]{0,1:T(8,128)S(1)} %get-tuple-element.73), channel_id=1, source_target_pairs={{0,4},{4,8},{8,12},{12,16},{16,20},{20,24},{24,28},{28,0},{1,5},{5... | collective-permute-start | bytes 6291464 | tf_op jit(solution)/shard_map/ppermute | solution.py:11
  192.4 1.3 copy-start.1
  198.0 161.2 %all-gather.11.cloned.1.call-start = ((), (), s32[]{:S(2)}) async-start(), calls=%async_computation.2 | async-start | bytes 1310720 | tf_op jit(solution)/shard_map/all_gather | solution.py:51
  288.9 50.5 %collective-permute-start.1 = (f32[4096,128]{0,1:T(8,128)S(1)}, f32[4096,128]{0,1:T(8,128)S(1)}, u32[]{:S(2)}, u32[]{:S(2)}) collective-permute-start(f32[4096,128]{0,1:T(8,128)S(1)} %get-tuple-element.71), channel_id=1, source_target_pairs={{0,4},{4,8},{8,12},{12,16},{16,20},{20,24},{24,28},{28,0},{1,5},{5... | collective-permute-start | bytes 6291464 | tf_op jit(solution)/shard_map/ppermute | solution.py:11
  339.5 1.3 copy-start
  365.4 0.7 copy-start.2
  439.3 65.3 %collective-permute-start.2 = (f32[4096,128]{0,1:T(8,128)}, f32[4096,128]{0,1:T(8,128)}, u32[]{:S(2)}, u32[]{:S(2)}) collective-permute-start(f32[4096,128]{0,1:T(8,128)} %get-tuple-element.69), channel_id=1, source_target_pairs={{0,4},{4,8},{8,12},{12,16},{16,20},{20,24},{24,28},{28,0},{1,5},{5... | collective-permute-start | bytes 6291464 | tf_op jit(solution)/shard_map/ppermute | solution.py:11
Sparse Core Ops, SparseCore 0:
  18.3 19.9 all-gather.6
  198.1 13.9 all-gather.8
  345.2 13.9 all-gather.10
